TPU v7x, 32 devices: a whole 2x2x4 slice. The times are simulated.
32 devices in a mesh: groups: 2 (over x), seq: 16 (over z, y, core).
Axes of the slice: x: 2, y: 2, z: 4, core: 2. Of those that a mesh axis runs over, the one named last changes fastest.
Arguments:
- clip_tokens: bfloat16 [32, 128, 512], P(('groups', 'seq')), parts along dimension 0, may hold values from -6 to 6
- spatial_qkv: bfloat16 [512, 1536], replicated, may hold values from -4.6403883 to 4.6403883
- spatial_out: bfloat16 [512, 512], replicated, may hold values from -0.5 to 0.5
- temporal_qkv: bfloat16 [512, 1536], replicated, may hold values from -4.6403883 to 4.6403883
- temporal_out: bfloat16 [512, 512], replicated, may hold values from -0.5 to 0.5
- mlp_up: bfloat16 [512, 2048], replicated, may hold values from -0.25 to 0.25
- mlp_down: bfloat16 [2048, 512], replicated, may hold values from -0.25 to 0.25
Outputs:
- layer_out: bfloat16 [32, 128, 512], P(('groups', 'seq')), parts along dimension 0
There are 2 independent parts, one for each index of `groups`. A program takes and returns all parts, laid end to end along the dimension named above; an argument that names none is the same for every part. Nothing has to cross between parts.
All inputs are finite; a program needn't handle non-finite values.
Results may differ from a plain program's by a relative error of at most 0.013.
Values may be sent and summed in bfloat16 or wider, within the bound.
A program may use at most 128 MiB of HBM per device.

v0:
```python
import functools
import math

import jax
import jax.numpy as jnp
from jax import lax
from jax.experimental import pallas as pl
from jax.experimental.pallas import tpu as pltpu
from jax.sharding import PartitionSpec as P

HEADS = 8
LANES = 128
VMEM_BYTES = 67043328
MESH = pl.DeviceIdType.MESH
F32 = jnp.float32
BF16 = jnp.bfloat16


def norm_rows(values):
    center = values - jnp.mean(values, axis=-1, keepdims=True)
    spread = jnp.mean(center * center, axis=-1, keepdims=True)
    return (center * lax.rsqrt(spread + 1e-05)).astype(BF16)


def gelu(u):
    return 0.5 * u * (1.0 + jnp.tanh(math.sqrt(2.0 / math.pi) * (u + 0.044715 * (u * u * u))))


def dot(a, b):
    return jnp.dot(a, b, preferred_element_type=F32)


def blocks_of(count, body):
    if count <= 2:
        for i in range(count):
            body(i)
    else:
        def step(i, carry):
            body(i)
            return carry

        lax.fori_loop(0, count, step, 0)


def attend(packed, first_row, rows, width, head_width, same_slot):
    total = packed.shape[0]
    per_block = LANES // head_width
    lane = lax.broadcasted_iota(jnp.int32, (rows, LANES), 1)
    ones = jnp.ones((total, LANES), BF16)
    scale = head_width ** (-0.5) * math.log2(math.e)
    if same_slot:
        query_at = lax.broadcasted_iota(jnp.int32, (per_block * rows, total), 0)
        key_at = lax.broadcasted_iota(jnp.int32, (per_block * rows, total), 1)
        allowed = lax.rem(query_at, same_slot) == lax.rem(key_at, same_slot)
    outs = []
    for block in range(width // LANES):
        q = packed[pl.ds(first_row, rows), pl.ds(block * LANES, LANES)]
        k = packed[:, pl.ds(width + block * LANES, LANES)]
        v = packed[:, pl.ds(2 * width + block * LANES, LANES)]
        split = [
            jnp.where((lane >= h * head_width) & (lane < (h + 1) * head_width), q, jnp.zeros_like(q))
            for h in range(per_block)
        ]
        scores = lax.dot_general(
            jnp.concatenate(split, axis=0), k, (((1,), (1,)), ((), ())), preferred_element_type=F32
        )
        if same_slot:
            scores = jnp.where(allowed, scores, -1e30)
        top = jnp.max(scores, axis=-1, keepdims=True)
        raised = jnp.exp2((scores - top) * scale).astype(BF16)
        both = dot(raised, jnp.concatenate([v, ones], axis=1))
        mixed = both[:, :LANES] / both[:, LANES:]
        out = mixed[:rows]
        for h in range(1, per_block):
            out = jnp.where(lane >= h * head_width, mixed[h * rows:(h + 1) * rows], out)
        outs.append(out.astype(BF16))
    return jnp.concatenate(outs, axis=1)


def kernel(
    n, x_hbm, wq1_hbm, wo1_hbm, wq2_hbm, wo2_hbm, up_hbm, down_hbm, out_v,
    x_v, wq1, wo1, wq2, wo2, up, down, packed, normed, send1, recv1, send2,
    load_sem, send1_sem, recv1_sem, send2_sem, recv2_sem,
):
    _, slot, width = x_v.shape
    total = n * slot
    head_width = width // HEADS
    half = n // 2
    me = lax.axis_index("seq")
    side = me // half
    near, far = side * half, (1 - side) * half
    place = lax.rem(me, half)

    def load(i, src, dst):
        return pltpu.make_async_copy(src, dst, load_sem.at[i])

    loads = [
        load(i, src, dst) for i, (src, dst) in enumerate(
            ((x_hbm, x_v), (wq1_hbm, wq1), (wo1_hbm, wo1), (wq2_hbm, wq2), (wo2_hbm, wo2), (up_hbm, up), (down_hbm, down))
        )
    ]
    bands = [pl.ds(b * width, width) for b in range(3)]
    band_loads = [load(i, wq1_hbm.at[:, band], wq1.at[:, band]) for i, band in zip((1, 7, 8), bands)]
    loads[0].start()
    for band_load in band_loads:
        band_load.start()

    def far_peer(j):
        return far + lax.rem(place + j, half)

    def near_peer(j):
        return near + lax.rem(place + j, half)

    def each(first, body):
        def step(j, carry):
            body(j)
            return carry

        lax.fori_loop(first, half, step, 0, unroll=half <= 8)

    barrier = pltpu.get_barrier_semaphore()
    each(0, lambda j: pl.semaphore_signal(barrier, inc=1, device_id={"seq": far_peer(j)}, device_id_type=MESH))
    each(1, lambda j: pl.semaphore_signal(barrier, inc=1, device_id={"seq": near_peer(j)}, device_id_type=MESH))

    def copy1(peer, source):
        return pltpu.make_async_remote_copy(
            src_ref=send1.at[peer], dst_ref=recv1.at[source], send_sem=send1_sem.at[peer],
            recv_sem=recv1_sem.at[source], device_id={"seq": peer}, device_id_type=MESH,
        )

    def copy2(peer, source):
        return pltpu.make_async_remote_copy(
            src_ref=send2.at[peer], dst_ref=out_v.at[source], send_sem=send2_sem.at[peer],
            recv_sem=recv2_sem.at[source], device_id={"seq": peer}, device_id_type=MESH,
        )

    def every_peer(body):
        each(0, lambda j: body(far_peer(j)))
        each(1, lambda j: body(near_peer(j)))

    row_block = min(128, total)
    slots_block = row_block // slot

    def project(source, weights, i):
        rows = source[pl.ds(i * slots_block, slots_block)].astype(F32).reshape(row_block, width)
        packed[pl.ds(i * row_block, row_block), :] = dot(norm_rows(rows), weights[...]).astype(BF16)

    part = min(64, half * slot)
    part_slots = part // slot
    parts = half // part_slots

    loads[0].wait()
    for i in range(2, 7):
        loads[i].start()

    def normalise(i):
        rows = x_v[pl.ds(i * slots_block, slots_block)].astype(F32).reshape(row_block, width)
        normed[pl.ds(i * row_block, row_block), :] = norm_rows(rows)

    def project_band(band, i):
        at = pl.ds(i * row_block, row_block)
        packed[at, band] = dot(normed[at, :], wq1[:, band]).astype(BF16)

    blocks_of(total // row_block, normalise)
    for band, band_load in zip(bands, band_loads):
        band_load.wait()
        blocks_of(total // row_block, functools.partial(project_band, band))

    def spatial(base, i):
        first = base + i * part_slots
        heads = attend(packed, pl.multiple_of(first * slot, part), part, width, head_width, 0)
        rows = x_v[pl.ds(first, part_slots)].astype(F32).reshape(part, width)
        merged = rows + dot(heads, wo1[...])
        send1[pl.ds(first, part_slots)] = merged.reshape(part_slots, slot, width).astype(BF16)

    loads[2].wait()
    blocks_of(parts, functools.partial(spatial, far))
    pl.semaphore_wait(barrier, n - 1)
    each(0, lambda j: copy1(far_peer(j), me).start())
    blocks_of(parts, functools.partial(spatial, near))
    each(1, lambda j: copy1(near_peer(j), me).start())
    recv1[me] = send1[me]

    for i in range(3, 7):
        loads[i].wait()
    every_peer(lambda peer: copy1(me, peer).wait_recv())
    blocks_of(total // row_block, functools.partial(project, recv1, wq2))

    def temporal(base, i):
        first = base + i * part_slots
        heads = attend(packed, pl.multiple_of(first * slot, part), part, width, head_width, slot)
        rows = recv1[pl.ds(first, part_slots)].astype(F32).reshape(part, width)
        after = (rows + dot(heads, wo2[...])).astype(BF16).astype(F32)
        hidden = gelu(dot(norm_rows(after), up[...])).astype(BF16)
        done = after + dot(hidden, down[...])
        send2[pl.ds(first, part_slots)] = done.reshape(part_slots, slot, width).astype(BF16)

    blocks_of(parts, functools.partial(temporal, far))
    each(0, lambda j: copy2(far_peer(j), me).start())
    blocks_of(parts, functools.partial(temporal, near))
    each(1, lambda j: copy2(near_peer(j), me).start())
    out_v[me] = send2[me]
    every_peer(lambda peer: copy1(peer, me).wait_send())
    every_peer(lambda peer: copy2(peer, me).wait_send())
    every_peer(lambda peer: copy2(me, peer).wait_recv())


def store(rows_v, out_hbm, sem):
    copy = pltpu.make_async_copy(rows_v, out_hbm, sem)
    copy.start()
    copy.wait()


def solution(mesh):
    n = mesh.shape["seq"]

    def local(clip_tokens, *weights):
        frames, patches, width = clip_tokens.shape
        assert frames == 1
        slot = patches // n
        blocks = (n, slot, width)
        vmem = [pltpu.VMEM(w.shape, w.dtype) for w in weights]
        out = pl.pallas_call(
            functools.partial(kernel, n),
            out_shape=pltpu.VMEM(blocks, BF16),
            in_specs=[pl.BlockSpec(memory_space=pltpu.HBM)] * 7,
            out_specs=pl.BlockSpec(memory_space=pltpu.VMEM),
            scratch_shapes=[
                pltpu.VMEM(blocks, BF16),
                *vmem,
                pltpu.VMEM((patches, 3 * width), BF16),
                pltpu.VMEM((patches, width), BF16),
                pltpu.VMEM(blocks, BF16),
                pltpu.VMEM(blocks, BF16),
                pltpu.VMEM(blocks, BF16),
                pltpu.SemaphoreType.DMA((9,)),
                pltpu.SemaphoreType.DMA((n,)),
                pltpu.SemaphoreType.DMA((n,)),
                pltpu.SemaphoreType.DMA((n,)),
                pltpu.SemaphoreType.DMA((n,)),
            ],
            compiler_params=pltpu.CompilerParams(collective_id=0, has_side_effects=True, vmem_limit_bytes=VMEM_BYTES - math.prod(blocks) * 2 - 65536),
            name="layer",
        )(clip_tokens.reshape(blocks), *weights)
        return out.reshape(frames, patches, width)

    in_specs = (P(("groups", "seq"), None, None), P(), P(), P(), P(), P(), P())
    out_specs = P(("groups", "seq"), None, None)
    return jax.shard_map(local, mesh=mesh, in_specs=in_specs, out_specs=out_specs, check_vma=False)
```

profile of v0, /device:TPU:0, one launch (start us, length us, event | category | flops | bytes accessed | tf_op | source)
XLA Modules:
  0.0 19.8 jit_solution(1521808431663847971)
XLA Ops:
  0.0 19.2 %layer.1 = bf16[16,8,512]{2,1,0:T(8,128)(2,1)S(1)} custom-call(bf16[16,8,512]{2,1,0:T(8,128)(2,1)} %bitcast.3, bf16[512,1536]{1,0:T(8,128)(2,1)} %wq1_hbm.1, bf16[512,512]{1,0:T(8,128)(2,1)} %wo1_hbm.1, bf16[512,1536]{1,0:T(8,128)(2,1)} %wq2_hbm.1, bf16[512,512]{1,0:T(8,128)(2,1)} %wo2_hbm.1, bf16[512,2048]{1,0:T(8,128)(2,1)} %up_hbm.1, ...), custom_call_target="tpu_custom_call" | custom-call | tf_op jit(solution)/shard_map/layer/pallas_call | solution.py:223
  19.2 0.7 %copy.9 = bf16[1,128,512]{2,1,0:T(8,128)(2,1)} copy(bf16[1,128,512]{2,1,0:T(8,128)(2,1)S(1)} %bitcast.2) | data formatting | bytes 262144
where the time goes:
time: 20 us; the launch traced here: 19.8 us
  Pallas kernels  19.2 us (96%)
  local copies, waits for them, and re-layouts  0.66 us (3%)
    pallas_call x1, Pallas kernels, local(): pl.pallas_call(functools.partial(kernel, n), out_shape=pltpu.VMEM(blocks,...  19.2 us
    unnamed x1, local copies, waits for them, and re-layouts  0.66 us

commit v1 on v0

v1 whole, which is shorter than its diff:
```python
import functools
import math

import jax
import jax.numpy as jnp
from jax import lax
from jax.experimental import pallas as pl
from jax.experimental.pallas import tpu as pltpu
from jax.sharding import PartitionSpec as P

HEADS = 8
LANES = 128
VMEM_BYTES = 67043328
SHARES = (1, 1, 2, 0)
ORDERS = ((2, 1, 0, 3), (2, 0, 1, 3), (0, 1, 2, 3), (2, 0, 1, 3))
QUARTERS = len(SHARES)
MESH = pl.DeviceIdType.MESH
F32 = jnp.float32
BF16 = jnp.bfloat16
S = jax.named_scope


def norm_rows(values):
    center = values - jnp.mean(values, axis=-1, keepdims=True)
    spread = jnp.mean(center * center, axis=-1, keepdims=True)
    return (center * lax.rsqrt(spread + 1e-05)).astype(BF16)


def gelu(u):
    return 0.5 * u * (1.0 + jnp.tanh(math.sqrt(2.0 / math.pi) * (u + 0.044715 * (u * u * u))))


def dot(a, b):
    return jnp.dot(a, b, preferred_element_type=F32)


def blocks_of(count, body):
    if count <= 2:
        for i in range(count):
            body(i)
    else:
        def step(i, carry):
            body(i)
            return carry

        lax.fori_loop(0, count, step, 0)


def attend(packed, query_row, keys, rows, width, head_width, same_slot):
    per_block = LANES // head_width
    total = sum(count for _, count in keys)
    lane = lax.broadcasted_iota(jnp.int32, (total, LANES), 1)
    own = [(lane >= h * head_width) & (lane < (h + 1) * head_width) for h in range(per_block)]
    ones = jnp.concatenate([jnp.where(mask, 1.0, 0.0).astype(BF16) for mask in own], axis=0)
    scale = head_width ** (-0.5) * math.log2(math.e)
    if same_slot:
        query_at = lax.broadcasted_iota(jnp.int32, (rows, total), 0)
        key_at = lax.broadcasted_iota(jnp.int32, (rows, total), 1)
        allowed = lax.rem(query_at, same_slot) == lax.rem(key_at, same_slot)

    def spread(block, band):
        at = pl.ds(band * width + block * LANES, LANES)
        values = jnp.concatenate([packed[pl.ds(first, count), at] for first, count in keys], axis=0)
        return jnp.concatenate([jnp.where(mask, values, jnp.zeros_like(values)) for mask in own], axis=0)

    scores, weights, outs = [], [], []
    for block in range(width // LANES):
        q = packed[pl.ds(query_row, rows), pl.ds(block * LANES, LANES)]
        scores.append(lax.dot_general(q, spread(block, 1), (((1,), (1,)), ((), ())), preferred_element_type=F32))
    for both in scores:
        raised = []
        for h in range(per_block):
            one = both[:, h * total:(h + 1) * total]
            if same_slot:
                one = jnp.where(allowed, one, -1e30)
            top = jnp.max(one, axis=-1, keepdims=True)
            raised.append(jnp.exp2((one - top) * scale).astype(BF16))
        weights.append(jnp.concatenate(raised, axis=1))
    for block, weight in enumerate(weights):
        both = dot(weight, jnp.concatenate([spread(block, 2), ones], axis=1))
        outs.append((both[:, :LANES] / both[:, LANES:]).astype(BF16))
    return jnp.concatenate(outs, axis=1)


def kernel(
    n, x_hbm, wq1_hbm, wo1_hbm, wq2_hbm, wo2_hbm, up_hbm, down_hbm, out_v,
    x_v, wq1, wo1, wq2, wo2, up, down, packed, send1, recv1, send2,
    load_sem, send1_sem, recv1_sem, send2_sem, recv2_sem,
):
    _, slot, width = x_v.shape
    total = n * slot
    head_width = width // HEADS
    quarter = n // QUARTERS
    starts = [sum(SHARES[:i]) * quarter for i in range(QUARTERS)]
    me = lax.axis_index("seq")
    mine = me // quarter
    place = lax.rem(me, quarter)

    loads = [
        pltpu.make_async_copy(src, dst, load_sem.at[i]) for i, (src, dst) in enumerate(
            ((x_hbm, x_v), (wq1_hbm, wq1), (wo1_hbm, wo1), (wq2_hbm, wq2), (wo2_hbm, wo2), (up_hbm, up), (down_hbm, down))
        )
    ]
    wide = 2 * width
    pair_load = pltpu.make_async_copy(wq1_hbm.at[:, pl.ds(0, wide)], wq1.at[:, pl.ds(0, wide)], load_sem.at[1])
    value_load = pltpu.make_async_copy(wq1_hbm.at[:, pl.ds(wide, width)], wq1.at[:, pl.ds(wide, width)], load_sem.at[7])
    loads[0].start()
    pair_load.start()
    value_load.start()
    loads[2].start()

    def each_of(group, body):
        def visit(j):
            at = lax.rem(place + j, quarter)
            body(group * quarter + at, at)

        @pl.when(mine != group)
        def _():
            visit(0)

        if quarter <= 8:
            for j in range(1, quarter):
                visit(j)
        else:
            def step(j, carry):
                visit(j)
                return carry

            lax.fori_loop(1, quarter, step, 0)

    barrier = pltpu.get_barrier_semaphore()

    def greet(peer, at):
        pl.semaphore_signal(barrier, inc=1, device_id={"seq": peer}, device_id_type=MESH)

    owners = [g for g in range(QUARTERS) if SHARES[g]]

    def if_owner(body):
        if len(owners) == QUARTERS:
            body()
        else:
            pl.when(functools.reduce(jnp.logical_or, [mine == g for g in owners]))(body)

    def greet_all():
        for g in range(QUARTERS):
            each_of(g, greet)

    if_owner(greet_all)

    def copy1(peer, source, at, s):
        return pltpu.make_async_remote_copy(
            src_ref=send1.at[source], dst_ref=recv1.at[s * n + at], send_sem=send1_sem,
            recv_sem=recv1_sem, device_id={"seq": peer}, device_id_type=MESH,
        )

    def copy2(peer, source, at):
        return pltpu.make_async_remote_copy(
            src_ref=send2.at[source], dst_ref=out_v.at[at], send_sem=send2_sem,
            recv_sem=recv2_sem, device_id={"seq": peer}, device_id_type=MESH,
        )

    def wait_bytes(buffer, count, sem):
        some = buffer.at[pl.ds(0, count)]
        pltpu.make_async_copy(some, some, sem).wait()

    row_block = min(128, total)
    block_slots = row_block // slot

    def project(source, weights, i, rows):
        values = source[pl.ds(i * (rows // slot), rows // slot)].astype(F32).reshape(rows, width)
        packed[pl.ds(i * rows, rows), :] = dot(norm_rows(values), weights[...]).astype(BF16)

    with S("xwait"):
        loads[0].wait()
    for i in range(3, 7):
        loads[i].start()

    def spatial(i):
        at = pl.ds(i * block_slots, block_slots)
        heads = attend(packed, i * row_block, [(0, total)], row_block, width, head_width, 0)
        merged = x_v[at].astype(F32).reshape(row_block, width) + dot(heads, wo1[...])
        send1[at] = merged.reshape(block_slots, slot, width).astype(BF16)

    with S("proj1"):
        if total == row_block:
            normed = norm_rows(x_v[...].astype(F32).reshape(total, width))
            pair_load.wait()
            packed[pl.ds(0, total), pl.ds(0, wide)] = dot(normed, wq1[:, pl.ds(0, wide)]).astype(BF16)
            value_load.wait()
            loads[2].wait()
            packed[pl.ds(0, total), pl.ds(wide, width)] = dot(normed, wq1[:, pl.ds(wide, width)]).astype(BF16)
            spatial(0)
        else:
            pair_load.wait()
            value_load.wait()
            loads[2].wait()
            blocks_of(total // row_block, lambda i: project(x_v, wq1, i, row_block))
            blocks_of(total // row_block, spatial)
    with S("barrier"):
        pl.semaphore_wait(barrier, len(owners) * quarter - functools.reduce(lambda a, b: a + b, [(mine == g).astype(jnp.int32) for g in owners]))

    def send_first(groups):
        for g in groups:
            def give(peer, at, g=g):
                for s in range(SHARES[g]):
                    copy1(peer, starts[g] + at * SHARES[g] + s, me, s).start()

            if SHARES[g]:
                each_of(g, give)

    for g in range(QUARTERS):
        pl.when(mine == g)(functools.partial(send_first, ORDERS[g]))

    with S("loads"):
        for i in range(3, 7):
            loads[i].wait()

    def first_slot(share):
        same = [g for g in range(QUARTERS) if SHARES[g] == share]
        base = starts[same[0]]
        for g in same[1:]:
            base = jnp.where(mine == g, starts[g], base)
        return base + place * share

    def temporal(share):
        span = share * total
        base = first_slot(share)
        for s in range(share):
            recv1[s * n + me] = send1[base + s]
        with S("recv1"):
            wait_bytes(recv1, share * (n - 1), recv1_sem)
        rows = span if total <= 128 else row_block
        with S("proj2"):
            blocks_of(span // rows, lambda i: project(recv1, wq2, i, rows))
        part = row_block // share
        frames = part // slot

        def joined(pieces):
            return pieces[0] if share == 1 else jnp.concatenate(pieces, axis=0)

        def block(i):
            ranges = [pl.ds(s * n + i * frames, frames) for s in range(share)]
            heads = joined([
                attend(packed, s * total + i * part, [(s * total, total)], part, width, head_width, slot)
                for s in range(share)
            ])
            values = joined([recv1[at].astype(F32).reshape(part, width) for at in ranges])
            after = (values + dot(heads, wo2[...])).astype(BF16).astype(F32)
            hidden = gelu(dot(norm_rows(after), up[...])).astype(BF16)
            done = after + dot(hidden, down[...])
            for s, at in enumerate(ranges):
                send2[at] = done[s * part:(s + 1) * part].reshape(frames, slot, width).astype(BF16)

            def give(j):
                peer = i * frames + j

                @pl.when(peer != me)
                def _():
                    for s in range(share):
                        copy2(peer, s * n + peer, base + s).start()

            for j in range(frames):
                give(j)

        with S("temp"):
            blocks_of(total // part, block)

        for s in range(share):
            out_v[base + s] = send2[s * n + me]
        with S("wsend"):
            wait_bytes(send1, n - share, send1_sem)
            wait_bytes(send2, share * (n - 1), send2_sem)
        with S("recv2"):
            wait_bytes(out_v, n - share, recv2_sem)

    def watch():
        with S("wsend"):
            wait_bytes(send1, n, send1_sem)
        with S("recv2"):
            wait_bytes(out_v, n, recv2_sem)

    for share in sorted(set(SHARES)):
        body = functools.partial(temporal, share) if share else watch
        pl.when(functools.reduce(jnp.logical_or, [mine == g for g in range(QUARTERS) if SHARES[g] == share]))(body)


def solution(mesh):
    n = mesh.shape["seq"]

    def local(clip_tokens, *weights):
        frames, patches, width = clip_tokens.shape
        assert frames == 1 and n % QUARTERS == 0
        slot = patches // n
        blocks = (n, slot, width)
        most = max(SHARES)
        held = (most * n, slot, width)
        vmem = [pltpu.VMEM(w.shape, w.dtype) for w in weights]
        out = pl.pallas_call(
            functools.partial(kernel, n),
            out_shape=pltpu.VMEM(blocks, BF16),
            in_specs=[pl.BlockSpec(memory_space=pltpu.HBM)] * 7,
            out_specs=pl.BlockSpec(memory_space=pltpu.VMEM),
            scratch_shapes=[
                pltpu.VMEM(blocks, BF16),
                *vmem,
                pltpu.VMEM((most * patches, 3 * width), BF16),
                pltpu.VMEM(blocks, BF16),
                pltpu.VMEM(held, BF16),
                pltpu.VMEM(held, BF16),
                pltpu.SemaphoreType.DMA((8,)),
                pltpu.SemaphoreType.DMA,
                pltpu.SemaphoreType.DMA,
                pltpu.SemaphoreType.DMA,
                pltpu.SemaphoreType.DMA,
            ],
            compiler_params=pltpu.CompilerParams(collective_id=0, has_side_effects=True, vmem_limit_bytes=VMEM_BYTES - math.prod(blocks) * 2 - 65536),
            name="layer",
        )(clip_tokens.reshape(blocks), *weights)
        return out.reshape(frames, patches, width)

    in_specs = (P(("groups", "seq"), None, None), P(), P(), P(), P(), P(), P())
    out_specs = P(("groups", "seq"), None, None)
    return jax.shard_map(local, mesh=mesh, in_specs=in_specs, out_specs=out_specs, check_vma=False)
```

time: 20 us -> 17.5 us (0.88)
  Pallas kernels: 19.2 us -> 16.6 us
    pallas_call x1, Pallas kernels: 19.2 us -> 16.6 us  [local(): pl.pallas_call(functools.partial(kernel, n), out_shape=pltpu.VMEM(blocks,...]
where the time goes in v1:
time: 17.5 us; the launch traced here: 17.3 us
  Pallas kernels  16.6 us (95%)
  local copies, waits for them, and re-layouts  0.66 us (4%)
    pallas_call x1, Pallas kernels, local(): pl.pallas_call(functools.partial(kernel, n), out_shape=pltpu.VMEM(blocks,...  16.6 us
    unnamed x1, local copies, waits for them, and re-layouts  0.66 us

profile of v1, /device:TPU:0, one launch (start us, length us, event | category | flops | bytes accessed | tf_op | source)
XLA Modules:
  0.0 17.3 jit_solution(10810579992425642373)
XLA Ops:
  0.0 16.6 %layer.1 = bf16[16,8,512]{2,1,0:T(8,128)(2,1)S(1)} custom-call(bf16[16,8,512]{2,1,0:T(8,128)(2,1)} %bitcast.3, bf16[512,1536]{1,0:T(8,128)(2,1)} %wq1_hbm.1, bf16[512,512]{1,0:T(8,128)(2,1)} %wo1_hbm.1, bf16[512,1536]{1,0:T(8,128)(2,1)} %wq2_hbm.1, bf16[512,512]{1,0:T(8,128)(2,1)} %wo2_hbm.1, bf16[512,2048]{1,0:T(8,128)(2,1)} %up_hbm.1, ...), custom_call_target="tpu_custom_call" | custom-call | tf_op jit(solution)/shard_map/layer/pallas_call | solution.py:298
  16.7 0.7 %copy.9 = bf16[1,128,512]{2,1,0:T(8,128)(2,1)} copy(bf16[1,128,512]{2,1,0:T(8,128)(2,1)S(1)} %bitcast.2) | data formatting | bytes 262144
